TPU v7x, 128 devices: a whole 4x4x4 slice. The times are simulated.
128 devices in a mesh: period: 4 (over x_hi, core), bus: 32 (over z, x_lo, y).
Axes of the slice: x: 4 (x_hi: 2, x_lo: 2; x = x_hi * 2 + x_lo), y: 4, z: 4, core: 2. Of those that a mesh axis runs over, the one named last changes fastest.
Arguments:
- gain: bfloat16 [4, 2048, 2048], P('period', 'bus'), may hold values from -0.15 to 1.15
- schur: bfloat16 [4, 2048, 2048], P('period', 'bus'), may hold values from -0.0625 to 0.0625
- inverse_blocks: bfloat16 [4, 10240, 320], P('period', 'bus'), may hold values from -0.3125 to 0.3125
- sensitivity: bfloat16 [10240, 2048], P('bus'), may hold values from -0.109375 to 0.109375
- residual_bus: float32 [4, 10240, 512], P('period', 'bus'), may hold values from -6 to 6
- unit_rhs: float32 [4, 2048, 512], P('period', 'bus'), may hold values from -6 to 6
- start_state: float32 [2048, 512], P('bus'), may hold values from -6 to 6
- active_set: int32 [4, 10240], P('period', 'bus'), may hold values 0 or 1
- unit_bus: int32 [2048], replicated, may hold values from 0 to 10239
Outputs:
- storage_path: float32 [4, 2048, 512], P('period', 'bus')
- costate: float32 [4, 2048, 512], P('period', 'bus')
- bus_update: float32 [4, 10240, 512], P('period', 'bus')
All inputs are finite; a program needn't handle non-finite values. No bound on the sum of `active_set` on one device may be relied on, other than what follows from the above.
Results may differ from a plain program's by a relative error of at most 0.008.
Values may be sent and summed in bfloat16 or wider, within the bound.
A program may use at most 64 MiB of HBM per device.

v0:
```python
import jax
import jax.numpy as jnp
from jax import lax
from jax.sharding import PartitionSpec as P


def passed_along(block, axis, distance):
    devices = range(lax.axis_size(axis))
    route = [(i - distance, i) for i in devices if i - distance in devices]
    return lax.ppermute(block, axis, route)


def body(
    gain,
    schur,
    inverse_blocks,
    sensitivity,
    residual_bus,
    unit_rhs,
    start_state,
    active_set,
    unit_bus,
):
    per_dev, unit_rows, total_units = gain.shape
    bus_rows = inverse_blocks.shape[1]
    rhs_cols = residual_bus.shape[2]
    groups = lax.axis_size("period")
    period_rank = lax.axis_index("period")
    bus_rank = lax.axis_index("bus")
    weighted = residual_bus * (1.0 + 3.0 * active_set[:, :, None].astype(jnp.float32))
    net_in = weighted.astype(jnp.bfloat16)
    bus_solve = jnp.einsum(
        "tij,tjr->tir", inverse_blocks, net_in, preferred_element_type=jnp.float32
    ).astype(jnp.bfloat16)
    solve_flat = jnp.transpose(bus_solve, (1, 0, 2)).reshape(bus_rows, per_dev * rhs_cols)
    reduced = lax.psum_scatter(
        lax.dot_general(
            sensitivity, solve_flat, (((0,), (0,)), ((), ())), preferred_element_type=jnp.float32
        ),
        "bus",
        scatter_dimension=0,
        tiled=True,
    )
    unit_right = unit_rhs + jnp.transpose(reduced.reshape(unit_rows, per_dev, rhs_cols), (1, 0, 2))
    blocks_count = 1
    block_cols = rhs_cols // blocks_count
    section_count = groups + blocks_count - 1
    costate = jnp.zeros((per_dev, unit_rows, rhs_cols), jnp.float32)
    outgoing = jnp.zeros((unit_rows, block_cols), jnp.float32)
    for section_index in range(section_count):
        incoming = passed_along(outgoing.astype(jnp.bfloat16), "period", -1).astype(outgoing.dtype)
        block_index = section_index - (groups - 1 - period_rank)
        is_valid = (block_index >= 0) & (block_index < blocks_count)
        later = incoming
        for local_step in reversed(range(per_dev)):
            rounded = later.astype(jnp.bfloat16)

            def transposed(row_start, row_count, weights=gain[local_step], vector=rounded):
                return lax.dot_general(
                    weights, vector, (((0,), (0,)), ((), ())), preferred_element_type=jnp.float32
                )

            summed = lax.psum_scatter(
                transposed(jnp.int32(0), unit_rows * lax.axis_size("bus")),
                "bus",
                scatter_dimension=0,
                tiled=True,
            )
            current = unit_right[local_step] + summed
            costate = jnp.where(is_valid, current[None], costate)
            later = current
        outgoing = later
    costate_round = costate.astype(jnp.bfloat16)
    bus_ids = bus_rank * bus_rows + jnp.arange(bus_rows, dtype=jnp.int32)
    placement = (unit_bus[None, :] == bus_ids[:, None]).astype(jnp.bfloat16)
    storage_path = jnp.zeros((per_dev, unit_rows, rhs_cols), jnp.float32)
    bus_update = jnp.zeros((per_dev, bus_rows, rhs_cols), jnp.float32)
    outgoing = jnp.zeros((unit_rows, block_cols), jnp.float32)
    for section_index in range(section_count):
        incoming = passed_along(outgoing.astype(jnp.bfloat16), "period", 1).astype(outgoing.dtype)
        block_index = section_index - period_rank
        is_valid = (block_index >= 0) & (block_index < blocks_count)
        current = jnp.where(period_rank == 0, start_state, incoming)
        local_step = 0
        rounded = current.astype(jnp.bfloat16)
        own_costate = costate_round[local_step]
        whole_state = lax.all_gather(rounded, "bus", axis=0, tiled=True)
        whole_costate = lax.all_gather(own_costate, "bus", axis=0, tiled=True)
        coupling = jnp.dot(schur[local_step], whole_costate, preferred_element_type=jnp.float32)
        injection = jnp.dot(placement, whole_state, preferred_element_type=jnp.float32)
        network = (weighted[local_step] - injection).astype(jnp.bfloat16)
        angle = jnp.dot(inverse_blocks[local_step], network, preferred_element_type=jnp.float32)
        advanced = (
            jnp.dot(gain[local_step], whole_state, preferred_element_type=jnp.float32) - coupling
        )
        storage_path = jnp.where(is_valid, advanced[None], storage_path)
        bus_update = jnp.where(is_valid, angle[None], bus_update)
        current = advanced
        outgoing = current
    return (storage_path, costate, bus_update)


def solution(mesh):
    placed = (
        P("period", "bus", None),
        P("period", "bus", None),
        P("period", "bus", None),
        P("bus", None),
        P("period", "bus", None),
        P("period", "bus", None),
        P("bus", None),
        P("period", "bus"),
        P(),
    )
    return jax.shard_map(
        body,
        mesh=mesh,
        in_specs=placed,
        out_specs=(P("period", "bus", None), P("period", "bus", None), P("period", "bus", None)),
        check_vma=False,
    )
```

profile of v0, /device:TPU:0, one launch (start us, length us, event | category | flops | bytes accessed | tf_op | source)
XLA Modules:
  0.0 1705.1 jit_solution(13985205716786645269)
XLA Ops:
  7.2 0.8 add_reduce_fusion
  8.0 0.5 copy-done
  8.5 4.9 convolution_bitcast_fusion.4
  13.4 5.3 copy.22
  18.8 0.0 reduce-scatter.18.cloned.1.call-start
  18.8 1.3 collective-permute-start.1
  20.1 1.8 collective-permute-done.1
  22.0 2.7 convolution_bitcast_fusion.3
  24.7 5.4 copy.24
  30.2 0.0 reduce-scatter.20.cloned.1.call-start
  30.2 159.3 %reduce-scatter.16.cloned.1.call-done = f32[64,512]{1,0:T(8,128)} async-done(((f32[2048,512]{1,0:T(8,128)}), f32[64,512]{1,0:T(8,128)}) %reduce-scatter.16.cloned.1.call-update) | async-done | bytes 131088 | tf_op jit(solution)/shard_map/reduce_scatter | solution.py:36
  189.6 167.7 %reduce-scatter.18.cloned.1.call-done = f32[64,512]{1,0:T(8,128)} async-done(((f32[2048,512]{1,0:T(8,128)}), f32[64,512]{1,0:T(8,128)}) %reduce-scatter.18.cloned.1.call-update) | async-done | bytes 131088 | tf_op jit(solution)/shard_map/reduce_scatter | solution.py:63
  357.3 1.0 fusion.91
  358.3 1.3 collective-permute-start.2
  359.6 1.8 collective-permute-done.2
  361.4 2.8 convolution_bitcast_fusion.2
  364.2 5.3 copy.26
  369.5 0.0 reduce-scatter.22.cloned.1.call-start
  369.6 166.2 %reduce-scatter.20.cloned.1.call-done = f32[64,512]{1,0:T(8,128)} async-done(((f32[2048,512]{1,0:T(8,128)}), f32[64,512]{1,0:T(8,128)}) %reduce-scatter.20.cloned.1.call-update) | async-done | bytes 131088 | tf_op jit(solution)/shard_map/reduce_scatter | solution.py:63
  535.8 0.9 fusion.92
  536.7 1.3 collective-permute-start.3
  538.0 1.8 collective-permute-done.3
  539.8 2.8 convolution_bitcast_fusion.1
  542.6 5.3 copy.28
  547.9 0.0 reduce-scatter.24.cloned.1.call-start
  548.0 165.6 %reduce-scatter.22.cloned.1.call-done = f32[64,512]{1,0:T(8,128)} async-done(((f32[2048,512]{1,0:T(8,128)}), f32[64,512]{1,0:T(8,128)}) %reduce-scatter.22.cloned.1.call-update) | async-done | bytes 131088 | tf_op jit(solution)/shard_map/reduce_scatter | solution.py:63
  713.6 0.9 fusion.93
  714.5 1.3 collective-permute-start.4
  715.8 1.8 collective-permute-done.4
  717.6 2.8 convolution_bitcast_fusion
  720.4 5.3 copy.30
  725.8 0.0 all-gather.8.cloned.1.call-start
  725.9 166.4 %reduce-scatter.24.cloned.1.call-done = f32[64,512]{1,0:T(8,128)} async-done(((f32[2048,512]{1,0:T(8,128)}), f32[64,512]{1,0:T(8,128)}) %reduce-scatter.24.cloned.1.call-update) | async-done | bytes 131088 | tf_op jit(solution)/shard_map/reduce_scatter | solution.py:63
  892.3 1.6 fusion.94
  894.0 0.0 all-gather.6.cloned.1.call-start
  894.0 1.3 collective-permute-start
  895.3 0.9 collective-permute-done
  896.2 0.6 select_convert_fusion.3
  896.9 0.0 all-gather.10.cloned.1.call-start
  896.9 146.7 %all-gather.8.cloned.1.call-done = bf16[2048,512]{1,0:T(8,128)(2,1)} async-done(((bf16[64,512]{1,0:T(8,128)(2,1)}), bf16[2048,512]{1,0:T(8,128)(2,1)}) %all-gather.8.cloned.1.call-update) | async-done | bytes 2097168 | tf_op jit(solution)/shard_map/all_gather | solution.py:88
  1043.7 2.1 fusion.74
  1045.7 153.3 %all-gather.6.cloned.1.call-done = bf16[2048,512]{1,0:T(8,128)(2,1)} async-done(((bf16[64,512]{1,0:T(8,128)(2,1)}), bf16[2048,512]{1,0:T(8,128)(2,1)}) %all-gather.6.cloned.1.call-update) | async-done | bytes 2097168 | tf_op jit(solution)/shard_map/all_gather | solution.py:87
  1199.1 2.1 convolution_subtract_fusion.3
  1201.2 1.3 collective-permute-start.5
  1202.5 0.9 collective-permute-done.5
  1203.3 0.6 select_convert_fusion.2
  1204.0 0.0 all-gather.12.cloned.1.call-start
  1204.1 158.0 %all-gather.10.cloned.1.call-done = bf16[2048,512]{1,0:T(8,128)(2,1)} async-done(((bf16[64,512]{1,0:T(8,128)(2,1)}), bf16[2048,512]{1,0:T(8,128)(2,1)}) %all-gather.10.cloned.1.call-update) | async-done | bytes 2097168 | tf_op jit(solution)/shard_map/all_gather | solution.py:87
  1362.1 2.1 convolution_subtract_fusion.2
  1364.2 1.4 collective-permute-start.6
  1365.7 0.9 collective-permute-done.6
  1366.6 0.6 select_convert_fusion.1
  1367.2 0.0 all-gather.14.cloned.1.call-start
  1367.3 158.0 %all-gather.12.cloned.1.call-done = bf16[2048,512]{1,0:T(8,128)(2,1)} async-done(((bf16[64,512]{1,0:T(8,128)(2,1)}), bf16[2048,512]{1,0:T(8,128)(2,1)}) %all-gather.12.cloned.1.call-update) | async-done | bytes 2097168 | tf_op jit(solution)/shard_map/all_gather | solution.py:87
  1525.3 2.1 convolution_subtract_fusion.1
  1527.4 1.3 collective-permute-start.7
  1528.7 0.9 collective-permute-done.7
  1529.6 0.6 select_convert_fusion
  1530.3 3.7 fusion.51
  1534.0 3.6 fusion.48
  1537.6 150.7 %all-gather.14.cloned.1.call-done = bf16[2048,512]{1,0:T(8,128)(2,1)} async-done(((bf16[64,512]{1,0:T(8,128)(2,1)}), bf16[2048,512]{1,0:T(8,128)(2,1)}) %all-gather.14.cloned.1.call-update) | async-done | bytes 2097168 | tf_op jit(solution)/shard_map/all_gather | solution.py:87
  1688.4 3.6 fusion.45
  1692.0 2.7 fusion.54
  1694.7 3.6 fusion.31
  (37 shorter events, 0.3 us)
Async XLA Ops:
  7.2 1.3 copy-start
  7.2 182.4 %reduce-scatter.16.cloned.1.call-start = ((), (), s32[]{:S(2)}) async-start(), calls=%async_computation.10 | async-start | bytes 4325376 | tf_op jit(solution)/shard_map/reduce_scatter | solution.py:36
  18.7 3.2 copy-start.1
  18.8 338.5 %reduce-scatter.18.cloned.1.call-start = ((), (), s32[]{:S(2)}) async-start(), calls=%async_computation.11 | async-start | bytes 4325376 | tf_op jit(solution)/shard_map/reduce_scatter | solution.py:63
  18.8 3.1 collective-permute-start.1
  30.2 327.1 %copy-start.9 = (f32[1,64,512]{2,1,0:T(8,128)S(1)}, f32[1,64,512]{2,1,0:T(8,128)}, u32[]{:S(2)}) copy-start(f32[1,64,512]{2,1,0:T(8,128)} %param.14) | copy-start | bytes 393220
  30.2 505.6 %reduce-scatter.20.cloned.1.call-start = ((), (), s32[]{:S(2)}) async-start(), calls=%async_computation.12 | async-start | bytes 4325376 | tf_op jit(solution)/shard_map/reduce_scatter | solution.py:63
  358.3 3.1 collective-permute-start.2
  369.5 344.0 %reduce-scatter.22.cloned.1.call-start = ((), (), s32[]{:S(2)}) async-start(), calls=%async_computation.13 | async-start | bytes 4325376 | tf_op jit(solution)/shard_map/reduce_scatter | solution.py:63
  536.7 3.1 collective-permute-start.3
  547.9 344.4 %reduce-scatter.24.cloned.1.call-start = ((), (), s32[]{:S(2)}) async-start(), calls=%async_computation.14 | async-start | bytes 4325376 | tf_op jit(solution)/shard_map/reduce_scatter | solution.py:63
  714.5 3.1 collective-permute-start.4
  725.7 166.6 %copy-start.4 = (f32[64,512]{1,0:T(8,128)S(1)}, f32[64,512]{1,0:T(8,128)}, u32[]{:S(2)}) copy-start(f32[64,512]{1,0:T(8,128)} %reduce-scatter.20.cloned.1.call-done) | copy-start | bytes 393220
  725.7 166.6 %copy-start.5 = (f32[64,512]{1,0:T(8,128)S(1)}, f32[64,512]{1,0:T(8,128)}, u32[]{:S(2)}) copy-start(f32[64,512]{1,0:T(8,128)} %reduce-scatter.22.cloned.1.call-done) | copy-start | bytes 393220
  725.7 166.6 %copy-start.6 = (f32[64,512]{1,0:T(8,128)S(1)}, f32[64,512]{1,0:T(8,128)}, u32[]{:S(2)}) copy-start(f32[64,512]{1,0:T(8,128)} %reduce-scatter.18.cloned.1.call-done) | copy-start | bytes 393220
  725.7 170.5 %copy-start.2 = (f32[64,512]{1,0:T(8,128)S(1)}, f32[64,512]{1,0:T(8,128)}, u32[]{:S(2)}) copy-start(f32[64,512]{1,0:T(8,128)} %param.15) | copy-start | bytes 393220
  725.7 317.9 %copy-start.7 = (bf16[1,64,2048]{2,1,0:T(8,128)(2,1)S(1)}, bf16[1,64,2048]{2,1,0:T(8,128)(2,1)}, u32[]{:S(2)}) copy-start(bf16[1,64,2048]{2,1,0:T(8,128)(2,1)} %param.10) | copy-start | bytes 786436
  725.8 317.9 %all-gather.8.cloned.1.call-start = ((), (), s32[]{:S(2)}) async-start(), calls=%async_computation.6 | async-start | bytes 2162688 | tf_op jit(solution)/shard_map/all_gather | solution.py:88
  894.0 305.1 %all-gather.6.cloned.1.call-start = ((), (), s32[]{:S(2)}) async-start(), calls=%async_computation.5 | async-start | bytes 2162688 | tf_op jit(solution)/shard_map/all_gather | solution.py:87
  894.0 2.2 collective-permute-start
  896.9 465.2 %all-gather.10.cloned.1.call-start = ((), (), s32[]{:S(2)}) async-start(), calls=%async_computation.7 | async-start | bytes 2162688 | tf_op jit(solution)/shard_map/all_gather | solution.py:87
  1201.2 2.2 collective-permute-start.5
  1204.0 321.3 %all-gather.12.cloned.1.call-start = ((), (), s32[]{:S(2)}) async-start(), calls=%async_computation.8 | async-start | bytes 2162688 | tf_op jit(solution)/shard_map/all_gather | solution.py:87
  1364.2 166.1 %copy-start.3 = (f32[1,320,512]{2,1,0:T(8,128)S(1)}, f32[1,320,512]{2,1,0:T(8,128)}, u32[]{:S(2)}) copy-start(f32[1,320,512]{2,1,0:T(8,128)} %param.13) | copy-start | bytes 1966084
  1364.2 166.1 %copy-start.8 = (bf16[1,320,320]{2,1,0:T(8,128)(2,1)S(1)}, bf16[1,320,320]{2,1,0:T(8,128)(2,1)}, u32[]{:S(2)}) copy-start(bf16[1,320,320]{2,1,0:T(8,128)(2,1)} %param.11) | copy-start | bytes 614404
  1364.2 166.1 %copy-start.10 = (s32[2048]{0:T(1024)S(1)}, s32[2048]{0:T(1024)}, u32[]{:S(2)}) copy-start(s32[2048]{0:T(1024)} %param.17) | copy-start | bytes 24580
  1364.2 2.3 collective-permute-start.6
  1367.2 321.1 %all-gather.14.cloned.1.call-start = ((), (), s32[]{:S(2)}) async-start(), calls=%async_computation.9 | async-start | bytes 2162688 | tf_op jit(solution)/shard_map/all_gather | solution.py:87
  1527.4 2.2 collective-permute-start.7
Sparse Core Ops, SparseCore 0:
  18.9 170.6 reduce-scatter.15
  191.9 165.2 reduce-scatter.17
  369.7 166.0 reduce-scatter.19
  548.1 165.4 reduce-scatter.21
  725.9 166.3 reduce-scatter.23
  894.4 149.2 all-gather.7
  1045.9 153.1 all-gather.5
  1204.1 157.9 all-gather.9
  1367.3 157.9 all-gather.11
  1530.4 157.9 all-gather.13
where the time goes:
time: 1710 us
  waiting for transfers between devices  1600 us (94%)
  matrix products  41.4 us (2%)
  local copies, waits for them, and re-layouts  27.3 us (2%)
    reduce_scatter x4, waiting for transfers between devices, body(): lax.psum_scatter(transposed(jnp.int32(0), unit_rows * lax.axis_size('bus'...  666 us
    all_gather x4, waiting for transfers between devices, body(): whole_state = lax.all_gather(rounded, 'bus', axis=0, tiled=True)  620 us
    reduce_scatter x1, waiting for transfers between devices, body(): lax.psum_scatter(lax.dot_general(sensitivity, solve_flat, (((0,), (0,)),...  159 us
    all_gather x1, waiting for transfers between devices, body(): whole_costate = lax.all_gather(own_costate, 'bus', axis=0, tiled=True)  147 us
  transfers between devices with their start and end apart: 18, of which 18 were waited for; matrix products, arithmetic and copies ran while one was open for 1% of the time, Pallas kernels for 0%

commit v1 on v0

--- a/solution.py
+++ b/solution.py
@@ -84,7 +84,9 @@
         local_step = 0
         rounded = current.astype(jnp.bfloat16)
         own_costate = costate_round[local_step]
-        whole_state = lax.all_gather(rounded, "bus", axis=0, tiled=True)
+        whole_state = jnp.concatenate(
+            lax.all_to_all(jnp.stack([rounded] * lax.axis_size("bus")), "bus", 0, 0), axis=0
+        )
         whole_costate = lax.all_gather(own_costate, "bus", axis=0, tiled=True)
         coupling = jnp.dot(schur[local_step], whole_costate, preferred_element_type=jnp.float32)
         injection = jnp.dot(placement, whole_state, preferred_element_type=jnp.float32)

time: 1710 us -> 1190 us (0.70)
  waiting for transfers between devices: 1600 us -> 1010 us
  blocking collectives: 0 us -> 68.3 us
    all_gather x4 -> x0, waiting for transfers between devices: 620 us -> none  [body(): whole_state = lax.all_gather(rounded, 'bus', axis=0, tiled=True)]
    all_to_all x0 -> x2, blocking collectives: none -> 68.3 us  [body(): lax.all_to_all(jnp.stack([rounded] * lax.axis_size('bus')), 'bus', 0, 0)]
    all_to_all x0 -> x2, waiting for transfers between devices: none -> 23 us  [body(): lax.all_to_all(jnp.stack([rounded] * lax.axis_size('bus')), 'bus', 0, 0)]
  transfers between devices with their start and end apart: 18 -> 16, of which waited for: 18 -> 15; matrix products, arithmetic and copies ran while one was open for 1% -> 2% of each run, Pallas kernels for 0% -> 0%
where the time goes in v1:
time: 1190 us
  waiting for transfers between devices  1010 us (85%)
  blocking collectives  68.3 us (6%)
  matrix products  38.3 us (3%)
  local copies, waits for them, and re-layouts  33.7 us (3%)
  starting transfers between devices  24.4 us (2%)
  between operations  14.4 us (1%)
    reduce_scatter x4, waiting for transfers between devices, body(): lax.psum_scatter(transposed(jnp.int32(0), unit_rows * lax.axis_size('bus'...  665 us
    reduce_scatter x1, waiting for transfers between devices, body(): lax.psum_scatter(lax.dot_general(sensitivity, solve_flat, (((0,), (0,)),...  160 us
    all_gather x1, waiting for transfers between devices, body(): whole_costate = lax.all_gather(own_costate, 'bus', axis=0, tiled=True)  147 us
    all_to_all x2, blocking collectives, body(): lax.all_to_all(jnp.stack([rounded] * lax.axis_size('bus')), 'bus', 0, 0)  68.3 us
    unnamed x33, local copies, waits for them, and re-layouts  30.1 us
  transfers between devices with their start and end apart: 16, of which 15 were waited for; matrix products, arithmetic and copies ran while one was open for 2% of the time, Pallas kernels for 0%

profile of v1, /device:TPU:0, one launch (start us, length us, event | category | flops | bytes accessed | tf_op | source)
XLA Modules:
  0.0 1190.5 jit_solution(438241025909549476)
XLA Ops:
  7.2 0.0 reduce-scatter.16.cloned.1.call-start
  7.2 0.8 add_reduce_fusion
  8.0 0.5 copy-done
  8.5 4.9 convolution_bitcast_fusion.4
  13.4 5.3 copy.22
  18.8 0.0 reduce-scatter.18.cloned.1.call-start
  18.8 1.3 collective-permute-start.1
  20.1 1.8 collective-permute-done.1
  22.0 2.7 convolution_bitcast_fusion.3
  24.7 5.5 copy.24
  30.2 0.0 reduce-scatter.20.cloned.1.call-start
  30.2 159.8 %reduce-scatter.16.cloned.1.call-done = f32[64,512]{1,0:T(8,128)} async-done(((f32[2048,512]{1,0:T(8,128)}), f32[64,512]{1,0:T(8,128)}) %reduce-scatter.16.cloned.1.call-update) | async-done | bytes 131088 | tf_op jit(solution)/shard_map/reduce_scatter | solution.py:36
  190.0 166.6 %reduce-scatter.18.cloned.1.call-done = f32[64,512]{1,0:T(8,128)} async-done(((f32[2048,512]{1,0:T(8,128)}), f32[64,512]{1,0:T(8,128)}) %reduce-scatter.18.cloned.1.call-update) | async-done | bytes 131088 | tf_op jit(solution)/shard_map/reduce_scatter | solution.py:63
  356.6 1.0 fusion.91
  357.6 1.3 collective-permute-start.2
  358.9 1.8 collective-permute-done.2
  360.7 2.8 convolution_bitcast_fusion.2
  363.5 5.3 copy.26
  368.9 0.0 reduce-scatter.22.cloned.1.call-start
  368.9 166.1 %reduce-scatter.20.cloned.1.call-done = f32[64,512]{1,0:T(8,128)} async-done(((f32[2048,512]{1,0:T(8,128)}), f32[64,512]{1,0:T(8,128)}) %reduce-scatter.20.cloned.1.call-update) | async-done | bytes 131088 | tf_op jit(solution)/shard_map/reduce_scatter | solution.py:63
  535.0 0.9 fusion.92
  535.9 1.3 collective-permute-start.3
  537.2 1.8 collective-permute-done.3
  539.1 2.8 convolution_bitcast_fusion.1
  541.8 5.3 copy.28
  547.2 0.0 reduce-scatter.24.cloned.1.call-start
  547.2 165.9 %reduce-scatter.22.cloned.1.call-done = f32[64,512]{1,0:T(8,128)} async-done(((f32[2048,512]{1,0:T(8,128)}), f32[64,512]{1,0:T(8,128)}) %reduce-scatter.22.cloned.1.call-update) | async-done | bytes 131088 | tf_op jit(solution)/shard_map/reduce_scatter | solution.py:63
  713.1 0.9 fusion.93
  714.0 1.3 collective-permute-start.4
  715.3 1.8 collective-permute-done.4
  717.2 2.8 convolution_bitcast_fusion
  720.0 5.3 copy.30
  725.3 0.0 all-gather.2.cloned.1.call-start
  725.4 166.3 %reduce-scatter.24.cloned.1.call-done = f32[64,512]{1,0:T(8,128)} async-done(((f32[2048,512]{1,0:T(8,128)}), f32[64,512]{1,0:T(8,128)}) %reduce-scatter.24.cloned.1.call-update) | async-done | bytes 131088 | tf_op jit(solution)/shard_map/reduce_scatter | solution.py:63
  891.7 1.6 fusion.94
  893.4 1.3 collective-permute-start
  894.7 0.9 collective-permute-done
  895.6 1.6 stack.8
  897.2 4.9 all-to-all-start
  902.1 147.3 %all-gather.2.cloned.1.call-done = bf16[2048,512]{1,0:T(8,128)(2,1)} async-done(((bf16[64,512]{1,0:T(8,128)(2,1)}), bf16[2048,512]{1,0:T(8,128)(2,1)}) %all-gather.2.cloned.1.call-update) | async-done | bytes 2097168 | tf_op jit(solution)/shard_map/all_gather | solution.py:90
  1049.4 2.1 fusion.74
  1051.4 2.1 convolution_subtract_fusion.3
  1053.5 1.3 collective-permute-start.5
  1054.8 0.9 collective-permute-done.5
  1055.7 0.2 stack.9
  1056.0 34.7 %all_to_all.20 = bf16[32,64,512]{2,1,0:T(8,128)(2,1)S(1)} all-to-all(bf16[32,64,512]{2,1,0:T(8,128)(2,1)S(1)} %stack.9), channel_id=1, replica_groups=mesh['period'=4,'bus'=32] {'bus'}, dimensions={0} | all-to-all | bytes 4194304 | tf_op jit(solution)/shard_map/all_to_all | solution.py:88
  1090.7 1.4 copy-done.3
  1092.1 0.5 convolution_subtract_fusion.2
  1092.6 2.7 collective-permute-start.6
  1095.3 0.9 collective-permute-done.6
  1096.2 0.2 stack.10
  1096.5 33.6 %all_to_all.21 = bf16[32,64,512]{2,1,0:T(8,128)(2,1)S(1)} all-to-all(bf16[32,64,512]{2,1,0:T(8,128)(2,1)S(1)} %stack.10), channel_id=1, replica_groups=mesh['period'=4,'bus'=32] {'bus'}, dimensions={0} | all-to-all | bytes 4194304 | tf_op jit(solution)/shard_map/all_to_all | solution.py:88
  1130.1 1.4 copy-done.4
  1131.5 0.5 convolution_subtract_fusion.1
  1132.0 2.6 collective-permute-start.7
  1134.6 0.9 collective-permute-done.7
  1135.5 1.6 stack.11
  1137.1 6.2 all-to-all-start.3
  1143.3 3.6 fusion.51
  1146.9 3.7 fusion.48
  1150.6 23.0 %all-to-all-done.3 = bf16[32,64,512]{2,1,0:T(8,128)(2,1)} async-done(((bf16[32,64,512]{2,1,0:T(8,128)(2,1)}), bf16[32,64,512]{2,1,0:T(8,128)(2,1)}, u32[]{:S(2)}, u32[]{:S(2)}) %all-to-all-start.3) | async-done | bytes 2097184 | tf_op jit(solution)/shard_map/all_to_all | solution.py:88
  1173.6 3.6 fusion.45
  1177.2 2.8 fusion.54
  1180.1 3.6 fusion.31
  (41 shorter events, 0.3 us)
Async XLA Ops:
  7.2 1.3 copy-start
  7.2 182.8 %reduce-scatter.16.cloned.1.call-start = ((), (), s32[]{:S(2)}) async-start(), calls=%async_computation.10 | async-start | bytes 4325376 | tf_op jit(solution)/shard_map/reduce_scatter | solution.py:36
  18.7 3.2 copy-start.2
  18.8 337.8 %reduce-scatter.18.cloned.1.call-start = ((), (), s32[]{:S(2)}) async-start(), calls=%async_computation.11 | async-start | bytes 4325376 | tf_op jit(solution)/shard_map/reduce_scatter | solution.py:63
  18.8 3.1 collective-permute-start.1
  30.2 326.4 %copy-start.12 = (f32[1,64,512]{2,1,0:T(8,128)S(1)}, f32[1,64,512]{2,1,0:T(8,128)}, u32[]{:S(2)}) copy-start(f32[1,64,512]{2,1,0:T(8,128)} %param.14) | copy-start | bytes 393220
  30.2 504.8 %reduce-scatter.20.cloned.1.call-start = ((), (), s32[]{:S(2)}) async-start(), calls=%async_computation.12 | async-start | bytes 4325376 | tf_op jit(solution)/shard_map/reduce_scatter | solution.py:63
  357.6 3.1 collective-permute-start.2
  368.9 344.3 %reduce-scatter.22.cloned.1.call-start = ((), (), s32[]{:S(2)}) async-start(), calls=%async_computation.13 | async-start | bytes 4325376 | tf_op jit(solution)/shard_map/reduce_scatter | solution.py:63
  535.9 3.1 collective-permute-start.3
  547.2 344.5 %reduce-scatter.24.cloned.1.call-start = ((), (), s32[]{:S(2)}) async-start(), calls=%async_computation.14 | async-start | bytes 4325376 | tf_op jit(solution)/shard_map/reduce_scatter | solution.py:63
  714.0 3.1 collective-permute-start.4
  725.3 166.4 %copy-start.7 = (f32[64,512]{1,0:T(8,128)S(1)}, f32[64,512]{1,0:T(8,128)}, u32[]{:S(2)}) copy-start(f32[64,512]{1,0:T(8,128)} %reduce-scatter.20.cloned.1.call-done) | copy-start | bytes 393220
  725.3 166.4 %copy-start.8 = (f32[64,512]{1,0:T(8,128)S(1)}, f32[64,512]{1,0:T(8,128)}, u32[]{:S(2)}) copy-start(f32[64,512]{1,0:T(8,128)} %reduce-scatter.22.cloned.1.call-done) | copy-start | bytes 393220
  725.3 166.4 %copy-start.9 = (f32[64,512]{1,0:T(8,128)S(1)}, f32[64,512]{1,0:T(8,128)}, u32[]{:S(2)}) copy-start(f32[64,512]{1,0:T(8,128)} %reduce-scatter.18.cloned.1.call-done) | copy-start | bytes 393220
  725.3 170.3 %copy-start.5 = (f32[64,512]{1,0:T(8,128)S(1)}, f32[64,512]{1,0:T(8,128)}, u32[]{:S(2)}) copy-start(f32[64,512]{1,0:T(8,128)} %param.15) | copy-start | bytes 393220
  725.3 324.0 %all-gather.2.cloned.1.call-start = ((), (), s32[]{:S(2)}) async-start(), calls=%async_computation.9 | async-start | bytes 2162688 | tf_op jit(solution)/shard_map/all_gather | solution.py:90
  893.4 2.2 collective-permute-start
  897.2 152.2 %copy-start.10 = (bf16[1,64,2048]{2,1,0:T(8,128)(2,1)S(1)}, bf16[1,64,2048]{2,1,0:T(8,128)(2,1)}, u32[]{:S(2)}) copy-start(bf16[1,64,2048]{2,1,0:T(8,128)(2,1)} %param.10) | copy-start | bytes 786436
  897.2 154.3 %all-to-all-start = ((bf16[32,64,512]{2,1,0:T(8,128)(2,1)}), bf16[32,64,512]{2,1,0:T(8,128)(2,1)}, u32[]{:S(2)}, u32[]{:S(2)}) async-start(bf16[32,64,512]{2,1,0:T(8,128)(2,1)} %stack.8), calls=%async_computation | async-start | bytes 4194304 | tf_op jit(solution)/shard_map/all_to_all | solution.py:88
  1053.5 2.2 collective-permute-start.5
  1090.7 1.4 copy-start.3
  1092.6 3.6 collective-permute-start.6
  1130.1 1.4 copy-start.4
  1132.0 3.5 collective-permute-start.7
  1137.1 6.2 copy-start.6
  1137.1 6.2 copy-start.11
  1137.1 6.2 copy-start.13
  1137.1 36.5 %all-to-all-start.3 = ((bf16[32,64,512]{2,1,0:T(8,128)(2,1)}), bf16[32,64,512]{2,1,0:T(8,128)(2,1)}, u32[]{:S(2)}, u32[]{:S(2)}) async-start(bf16[32,64,512]{2,1,0:T(8,128)(2,1)} %stack.11), calls=%async_computation.3 | async-start | bytes 4194304 | tf_op jit(solution)/shard_map/all_to_all | solution.py:88
  1177.2 6.4 copy-start.1
Sparse Core Ops, SparseCore 0:
  18.9 171.0 reduce-scatter.15
  192.4 164.1 reduce-scatter.17
  369.0 165.9 reduce-scatter.19
  547.3 165.7 reduce-scatter.21
  725.4 166.2 reduce-scatter.23
  893.8 155.5 all-gather.1
